TPU v7x, 128 devices: a whole 4x4x4 slice. The times are simulated.
128 devices in a mesh: dp: 8 (over z_hi, y), tensor: 4 (over z_lo, core), replica: 4 (over x).
Axes of the slice: x: 4, y: 4, z: 4 (z_hi: 2, z_lo: 2; z = z_hi * 2 + z_lo), core: 2. Of those that a mesh axis runs over, the one named last changes fastest.
Arguments:
- queries: bfloat16 [8192, 8192], P(('dp', 'replica'), 'tensor'), may hold values from -8 to 8
- d_out: bfloat16 [8192, 8192], P(('dp', 'replica'), 'tensor'), may hold values from -48 to 48
- conv_keys: bfloat16 [8192, 1024], P(('dp', 'replica'), 'tensor'), may hold values from -12 to 12
- conv_values: bfloat16 [8192, 1024], P(('dp', 'replica'), 'tensor'), may hold values from -6 to 6
- segment_ids: int32 [32, 256], P(('dp', 'replica')), may hold values from 0 to 3, never falling along the last dimension, each value on 1 to 192 neighbouring positions
- master_keys: float32 [4096, 1024], P('dp', 'tensor'), may hold values from -8 to 8
- master_values: float32 [4096, 1024], P('dp', 'tensor'), may hold values from -6 to 6
- moment_keys: float32 [4096, 1024], P('dp', 'tensor'), may hold values from -3 to 3
- moment_values: float32 [4096, 1024], P('dp', 'tensor'), may hold values from -3 to 3
- second_keys: float32 [4096, 1024], P('dp', 'tensor'), may hold values from 0.01 to 1
- second_values: float32 [4096, 1024], P('dp', 'tensor'), may hold values from 0.01 to 1
Outputs:
- new_master_keys: float32 [4096, 1024], P('dp', 'tensor')
- new_master_values: float32 [4096, 1024], P('dp', 'tensor')
- new_moment_keys: float32 [4096, 1024], P('dp', 'tensor')
- new_moment_values: float32 [4096, 1024], P('dp', 'tensor')
- new_second_keys: float32 [4096, 1024], P('dp', 'tensor')
- new_second_values: float32 [4096, 1024], P('dp', 'tensor')
- served_keys: bfloat16 [4096, 1024], P(None, 'tensor')
- served_values: bfloat16 [4096, 1024], P(None, 'tensor')
- grad_keys: float32 [4096, 1024], P('dp', 'tensor')
- grad_values: float32 [4096, 1024], P('dp', 'tensor')
Inputs may be any that keep to these rules, and one draw needn't show every extreme that they name: `segment_ids`: each row holds the conversation numbers of one device's 256 tokens.
All inputs are finite; a program needn't handle non-finite values.
Results may differ from a plain program's by a relative error of at most 0.0065.
Values may be sent and summed in bfloat16 or wider, within the bound.
No kernel may reach another device: no remote copies, remote signals or barrier semaphores. Data moves between devices by JAX's collectives and lax.ppermute only.
A program may use at most 256 MiB of HBM per device.

v0:
```python
import jax
import jax.numpy as jnp
from jax import lax
from jax.sharding import PartitionSpec as P

Q_HEADS = 64
KV_HEADS = 8
HEAD_DIM = 128
STEP = 20
BETA_ONE = 0.9
BETA_TWO = 0.95
LEARN_RATE = 0.05
WEIGHT_DECAY = 0.1
EPSILON = 1e-08


def sent_together(arrays, axis, dim, along):
    both = jnp.concatenate(arrays, axis=along)
    filled, at, done = (lax.psum_scatter(both, axis, scatter_dimension=dim, tiled=True), 0, [])
    for a in arrays:
        done.append(lax.slice_in_dim(filled, at, at + a.shape[along], axis=along))
        at += a.shape[along]
    return tuple(done)


def from_everyone(value, axis):
    copies = jnp.broadcast_to(value, (lax.axis_size(axis), *value.shape))
    return lax.all_to_all(copies, axis, split_axis=0, concat_axis=0, tiled=True)


def of_everyone(value, axis):
    everything = from_everyone(value, axis)
    return jnp.sum(everything, axis=0)


def in_one(arrays, axis):
    ends = [0]
    for a in arrays:
        ends.append(ends[-1] + a.size)
    subtotal = of_everyone(jnp.concatenate([a.ravel() for a in arrays]), axis)
    return tuple((subtotal[b:e].reshape(a.shape) for a, b, e in zip(arrays, ends, ends[1:])))


def side_by_side(arrays, axis, dim, along):
    ends, at = ([], 0)
    for a in arrays[:-1]:
        at += a.shape[along]
        ends.append(at)
    both = jnp.concatenate(arrays, axis=along)
    return tuple(jnp.split(lax.all_gather(both, axis, axis=dim, tiled=True), ends, axis=along))


def attend_block(query_rows, grad_rows, own_keys, own_values, cart_keys, cart_values, visible):
    tokens_here, head_dim = own_keys.shape
    heads_here = query_rows.shape[1] // head_dim
    factor = head_dim ** (-0.5)
    flat_query = query_rows.reshape(tokens_here * heads_here, head_dim)
    flat_grad = grad_rows.reshape(tokens_here * heads_here, head_dim)
    cart_scores = jnp.dot(flat_query, cart_keys.T, preferred_element_type=jnp.float32) * factor
    own_scores = jnp.dot(flat_query, own_keys.T, preferred_element_type=jnp.float32) * factor
    own_scores = own_scores.reshape(tokens_here, heads_here, tokens_here)
    own_scores = jnp.where(visible[:, None, :], own_scores, -jnp.inf).reshape(
        tokens_here * heads_here, tokens_here
    )
    highest = jnp.maximum(jnp.max(cart_scores, axis=1), jnp.max(own_scores, axis=1))[:, None]
    cart_exp = jnp.exp(cart_scores - highest)
    own_exp = jnp.exp(own_scores - highest)
    denominator = jnp.sum(cart_exp, axis=1, keepdims=True) + jnp.sum(own_exp, axis=1, keepdims=True)
    cart_probs = cart_exp / denominator
    own_probs = own_exp / denominator
    cart_dprob = jnp.dot(flat_grad, cart_values.T, preferred_element_type=jnp.float32)
    own_dprob = jnp.dot(flat_grad, own_values.T, preferred_element_type=jnp.float32)
    centre = jnp.sum(cart_probs * cart_dprob, axis=1, keepdims=True) + jnp.sum(
        own_probs * own_dprob, axis=1, keepdims=True
    )
    cart_dscore = (cart_probs * (cart_dprob - centre)).astype(jnp.bfloat16)
    contract = (((0,), (0,)), ((), ()))
    grad_values = lax.dot_general(
        cart_probs.astype(jnp.bfloat16), flat_grad, contract, preferred_element_type=jnp.float32
    )
    grad_keys = (
        lax.dot_general(cart_dscore, flat_query, contract, preferred_element_type=jnp.float32)
        * factor
    )
    return (grad_keys, grad_values)


def device_grads(queries, d_out, conv_keys, conv_values, cart_keys, cart_values, segments):
    tokens_here = conv_keys.shape[0]
    head_dim = HEAD_DIM
    group_size = Q_HEADS // KV_HEADS
    half_size = group_size // 2
    kv_local = conv_keys.shape[1] // head_dim
    places = jnp.arange(tokens_here, dtype=jnp.int32)
    visible = (segments[:, None] == segments[None, :]) & (places[None, :] <= places[:, None])
    key_parts = []
    value_parts = []
    for kv_head in range(kv_local):
        col_lo = kv_head * head_dim
        col_hi = col_lo + head_dim
        key_sum = jnp.zeros((cart_keys.shape[0], head_dim), jnp.float32)
        value_sum = jnp.zeros((cart_keys.shape[0], head_dim), jnp.float32)
        for which_half in range(2):
            start_col = (kv_head * group_size + which_half * half_size) * head_dim
            end_col = start_col + half_size * head_dim
            grad_keys, grad_values = attend_block(
                queries[:, start_col:end_col],
                d_out[:, start_col:end_col],
                conv_keys[:, col_lo:col_hi],
                conv_values[:, col_lo:col_hi],
                cart_keys[:, col_lo:col_hi],
                cart_values[:, col_lo:col_hi],
                visible,
            )
            key_sum = key_sum + grad_keys
            value_sum = value_sum + grad_values
        key_parts.append(key_sum)
        value_parts.append(value_sum)
    return (jnp.concatenate(key_parts, axis=1), jnp.concatenate(value_parts, axis=1))


def adamw_step(param, moment, second, grad):
    moment_new = BETA_ONE * moment + (1.0 - BETA_ONE) * grad
    second_new = BETA_TWO * second + (1.0 - BETA_TWO) * grad * grad
    moment_hat = moment_new / (1.0 - BETA_ONE**STEP)
    second_hat = second_new / (1.0 - BETA_TWO**STEP)
    param_new = param - LEARN_RATE * (
        moment_hat / (jnp.sqrt(second_hat) + EPSILON) + WEIGHT_DECAY * param
    )
    return (param_new, moment_new, second_new)


def per_device(
    queries,
    d_out,
    conv_keys,
    conv_values,
    segment_ids,
    master_keys,
    master_values,
    moment_keys,
    moment_values,
    second_keys,
    second_values,
):
    cart_keys, cart_values = (
        lax.all_gather(master_keys.astype(jnp.bfloat16), "dp", axis=0, tiled=True),
        lax.all_gather(master_values.astype(jnp.bfloat16), "dp", axis=0, tiled=True),
    )
    grad_keys, grad_values = device_grads(
        queries, d_out, conv_keys, conv_values, cart_keys, cart_values, segment_ids[0]
    )
    key_share, value_share = sent_together((grad_keys, grad_values), "dp", 0, 1)
    shard_keys, shard_values = in_one((key_share, value_share), "replica")
    new_master_keys, new_moment_keys, new_second_keys = adamw_step(
        master_keys, moment_keys, second_keys, shard_keys
    )
    new_master_values, new_moment_values, new_second_values = adamw_step(
        master_values, moment_values, second_values, shard_values
    )
    served_keys, served_values = side_by_side(
        (new_master_keys.astype(jnp.bfloat16), new_master_values.astype(jnp.bfloat16)), "dp", 0, 1
    )
    return (
        new_master_keys,
        new_master_values,
        new_moment_keys,
        new_moment_values,
        new_second_keys,
        new_second_values,
        served_keys,
        served_values,
        shard_keys,
        shard_values,
    )


def solution(mesh):
    return jax.shard_map(
        per_device,
        mesh=mesh,
        in_specs=(
            P(("dp", "replica"), "tensor"),
            P(("dp", "replica"), "tensor"),
            P(("dp", "replica"), "tensor"),
            P(("dp", "replica"), "tensor"),
            P(("dp", "replica"), None),
            P("dp", "tensor"),
            P("dp", "tensor"),
            P("dp", "tensor"),
            P("dp", "tensor"),
            P("dp", "tensor"),
            P("dp", "tensor"),
        ),
        out_specs=(
            P("dp", "tensor"),
            P("dp", "tensor"),
            P("dp", "tensor"),
            P("dp", "tensor"),
            P("dp", "tensor"),
            P("dp", "tensor"),
            P(None, "tensor"),
            P(None, "tensor"),
            P("dp", "tensor"),
            P("dp", "tensor"),
        ),
        check_vma=False,
    )
```

profile of v0, /device:TPU:0, one launch (start us, length us, event | category | flops | bytes accessed | tf_op | source)
XLA Modules:
  0.0 544.8 jit_solution(12731431613612274478)
XLA Ops:
  7.2 1.8 convert_element_type.36
  9.1 1.8 convert_element_type.37
  11.0 0.9 fusion.64
  11.8 0.2 broadcast_in_dim.28
  12.1 0.2 broadcast_in_dim.29
  12.3 0.3 copy.33
  12.6 1.3 fusion.88
  13.9 0.2 reshape.191
  14.1 0.2 reshape.193
  14.3 0.2 reshape.197
  14.5 0.2 reshape.195
  14.7 1.4 fusion.89
  16.0 0.9 reshape.192
  16.9 0.9 reshape.194
  17.7 0.9 reshape.198
  18.6 0.9 reshape.196
  19.5 1.2 fusion.91
  20.7 1.3 fusion.90
  21.9 2.2 fusion.92
  24.2 1.3 fusion.93
  25.5 43.1 %all-gather.4.cloned.1.call-done = bf16[4096,256]{1,0:T(8,128)(2,1)} async-done(((bf16[512,256]{1,0:T(8,128)(2,1)}), bf16[4096,256]{1,0:T(8,128)(2,1)}) %all-gather.4.cloned.1.call-update) | async-done | bytes 2097168 | tf_op jit(solution)/shard_map/all_gather | solution.py:147
  68.6 9.5 %multiply_reduce_fusion.5 = (f32[1024]{0:T(1024)S(1)}, f32[1024,4096]{1,0:T(8,128)}) fusion(bf16[1024,128]{1,0:T(8,128)(2,1)} %copy-done.15, bf16[4096,256]{1,0:T(8,128)(2,1)} %all-gather.4.cloned.1.call-done), kind=kOutput, calls=%fused_computation.13 | convolution fusion | flops 1082129408 | bytes 18092032 | tf_op jit(solution)/shard_map/dot_general | solution.py:59
  78.1 0.2 fusion.44
  78.3 8.9 %fusion.5 = f32[1024]{0:T(1024)S(1)} fusion(f32[1024,4096]{1,0:T(8,128)} %get-tuple-element.37, f32[1024]{0:T(1024)S(1)} %max.30), kind=kLoop, calls=%fused_computation.21 | loop fusion | flops 12581888 | bytes 16785408 | tf_op jit(solution)/shard_map/reduce_sum | solution.py:68
  87.2 8.1 %multiply_reduce_fusion.4 = (f32[1024]{0:T(1024)S(1)}, f32[1024,4096]{1,0:T(8,128)}) fusion(bf16[1024,128]{1,0:T(8,128)(2,1)S(1)} %reshape.197, bf16[4096,256]{1,0:T(8,128)(2,1)S(1)} %copy-done), kind=kOutput, calls=%fused_computation.12 | convolution fusion | flops 1082129408 | bytes 18092032 | tf_op jit(solution)/shard_map/dot_general | solution.py:59
  95.3 0.2 fusion.45
  95.5 8.9 %fusion.7 = f32[1024]{0:T(1024)S(1)} fusion(f32[1024,4096]{1,0:T(8,128)} %get-tuple-element.33, f32[1024]{0:T(1024)S(1)} %max.31), kind=kLoop, calls=%fused_computation.23 | loop fusion | flops 12581888 | bytes 16785408 | tf_op jit(solution)/shard_map/reduce_sum | solution.py:68
  104.4 8.1 %multiply_reduce_fusion.6 = (f32[1024]{0:T(1024)S(1)}, f32[1024,4096]{1,0:T(8,128)}) fusion(bf16[1024,128]{1,0:T(8,128)(2,1)S(1)} %reshape.193, bf16[4096,256]{1,0:T(8,128)(2,1)S(1)} %copy-done), kind=kOutput, calls=%fused_computation.14 | convolution fusion | flops 1082129408 | bytes 18092032 | tf_op jit(solution)/shard_map/dot_general | solution.py:59
  112.5 0.2 fusion.43
  112.7 8.9 %fusion.3 = f32[1024]{0:T(1024)S(1)} fusion(f32[1024,4096]{1,0:T(8,128)} %get-tuple-element.41, f32[1024]{0:T(1024)S(1)} %max.29), kind=kLoop, calls=%fused_computation.19 | loop fusion | flops 12581888 | bytes 16785408 | tf_op jit(solution)/shard_map/reduce_sum | solution.py:68
  121.6 9.7 %fusion.12 = f32[4096,128]{0,1:T(8,128)} fusion(bf16[1024,128]{1,0:T(8,128)(2,1)S(1)} %copy-done.27, f32[1024,4096]{1,0:T(8,128)} %get-tuple-element.33, f32[1024]{0:T(1024)S(1)} %add.109, f32[1024]{0:T(1024)S(1)} %max.31), kind=kOutput, calls=%fused_computation.29 | convolution fusion | flops 1090519040 | bytes 19144704 | tf_op jit(solution)/shard_map/dot_general | solution.py:78
  131.4 0.4 slice-done.3
  131.8 5.2 fusion.16
  137.0 8.1 %multiply_reduce_fusion.7 = (f32[1024]{0:T(1024)S(1)}, f32[1024,4096]{1,0:T(8,128)}) fusion(bf16[1024,128]{1,0:T(8,128)(2,1)S(1)} %reshape.191, bf16[4096,256]{1,0:T(8,128)(2,1)S(1)} %copy-done.1), kind=kOutput, calls=%fused_computation.15 | convolution fusion | flops 1082129408 | bytes 18092032 | tf_op jit(solution)/shard_map/dot_general | solution.py:59
  145.1 8.8 %fusion.1 = f32[1024]{0:T(1024)S(1)} fusion(f32[1024,4096]{1,0:T(8,128)} %get-tuple-element.45, f32[1024]{0:T(1024)S(1)} %max.28), kind=kLoop, calls=%fused_computation.17 | loop fusion | flops 12581888 | bytes 16785408 | tf_op jit(solution)/shard_map/reduce_sum | solution.py:68
  154.0 11.9 %fusion.31 = f32[4096,128]{0,1:T(8,128)} fusion(f32[4096,128]{0,1:T(8,128)} %fusion.12, bf16[1024,128]{1,0:T(8,128)(2,1)} %reshape.196, f32[1024,4096]{1,0:T(8,128)} %get-tuple-element.37, f32[1024]{0:T(1024)S(1)} %add.107, f32[1024]{0:T(1024)S(1)} %max.30), kind=kOutput, calls=%fused_computation.46 | convolution fusion | flops 1091043328 | bytes 21241856 | tf_op jit(solution)/shard_map/dot_general | solution.py:78
  165.9 0.2 fusion.42
  166.1 0.3 fusion.40
  166.5 0.9 fusion.41
  167.4 0.9 fusion.39
  168.3 0.9 fusion.38
  169.3 5.3 fusion.28
  174.6 11.8 %multiply_reduce_fusion.1 = (f32[1024]{0:T(1024)S(1)}, f32[1024,4096]{1,0:T(8,128)}) fusion(f32[1024]{0:T(1024)S(1)} %add.107, f32[1024]{0:T(1024)S(1)} %max.30, f32[1024,4096]{1,0:T(8,128)} %get-tuple-element.37, bf16[1024,128]{1,0:T(8,128)(2,1)S(1)} %copy-done.30, bf16[4096,256]{1,0:T(8,128)(2,1)} %all-gather.6.cloned.1.call-done), kind=kOutput, calls=%fused_computation.4 | convolution fusion | flops 1094712320 | bytes 34877440 | tf_op jit(solution)/shard_map/dot_general | solution.py:71
  186.4 14.7 %fusion.10 = f32[4096,128]{0,1:T(8,128)} fusion(bf16[1024,128]{1,0:T(8,128)(2,1)S(1)} %copy-done.16, f32[1024,4096]{1,0:T(8,128)} %get-tuple-element.49, f32[1024]{0:T(1024)S(1)} %add.108, f32[1024,4096]{1,0:T(8,128)} %get-tuple-element.37, f32[1024]{0:T(1024)S(1)} %add.107, f32[1024]{0:T(1024)S(1)} %max.30), kind=kOutput, calls=%fused_computation.26 | convolution fusion | flops 1098907648 | bytes 35926016 | tf_op jit(solution)/shard_map/dot_general | solution.py:82
  201.1 12.0 %multiply_reduce_fusion = (f32[1024]{0:T(1024)S(1)}, f32[1024,4096]{1,0:T(8,128)}) fusion(f32[1024]{0:T(1024)S(1)} %add.109, f32[1024]{0:T(1024)S(1)} %max.31, f32[1024,4096]{1,0:T(8,128)} %get-tuple-element.33, bf16[1024,128]{1,0:T(8,128)(2,1)S(1)} %copy-done.28, bf16[4096,256]{1,0:T(8,128)(2,1)} %all-gather.6.cloned.1.call-done), kind=kOutput, calls=%fused_computation.1 | convolution fusion | flops 1094712320 | bytes 34877440 | tf_op jit(solution)/shard_map/dot_general | solution.py:71
  213.2 9.3 %multiply_reduce_fusion.3 = (f32[1024]{0:T(1024)S(1)}, f32[1024,4096]{1,0:T(8,128)}) fusion(f32[1024]{0:T(1024)S(1)} %add.102, f32[1024]{0:T(1024)S(1)} %max.28, f32[1024,4096]{1,0:T(8,128)S(1)} %bitcast.34, bf16[1024,128]{1,0:T(8,128)(2,1)S(1)} %copy-done.26, bf16[4096,256]{1,0:T(8,128)(2,1)} %all-gather.6.cloned.1.call-done), kind=kOutput, calls=%fused_computation.10 | convolution fusion | flops 1094712320 | bytes 34877440 | tf_op jit(solution)/shard_map/dot_general | solution.py:71
  222.6 14.7 %fusion.8 = f32[4096,128]{0,1:T(8,128)} fusion(bf16[1024,128]{1,0:T(8,128)(2,1)S(1)} %copy-done.14, f32[1024,4096]{1,0:T(8,128)} %get-tuple-element.53, f32[1024]{0:T(1024)S(1)} %add.103, f32[1024,4096]{1,0:T(8,128)} %get-tuple-element.45, f32[1024]{0:T(1024)S(1)} %add.102, f32[1024]{0:T(1024)S(1)} %max.28), kind=kOutput, calls=%fused_computation.24 | convolution fusion | flops 1098907648 | bytes 35926016 | tf_op jit(solution)/shard_map/dot_general | solution.py:82
  237.3 11.6 %multiply_reduce_fusion.2 = (f32[1024]{0:T(1024)S(1)}, f32[1024,4096]{1,0:T(8,128)}) fusion(f32[1024]{0:T(1024)S(1)} %copy-done.34, f32[1024]{0:T(1024)S(1)} %copy-done.32, f32[1024,4096]{1,0:T(8,128)} %get-tuple-element.41, bf16[1024,128]{1,0:T(8,128)(2,1)S(1)} %copy-done.25, bf16[4096,256]{1,0:T(8,128)(2,1)S(1)} %copy-done.38), kind=kOutput, calls=%fused_computation.7 | convolution fusion | flops 1094712320 | bytes 34877440 | tf_op jit(solution)/shard_map/dot_general | solution.py:71
  249.0 13.7 %fusion.27 = f32[4096,128]{0,1:T(8,128)S(1)} fusion(f32[4096,128]{0,1:T(8,128)S(1)} %copy-done.40, bf16[1024,128]{1,0:T(8,128)(2,1)S(1)} %copy-done.12, f32[1024,4096]{1,0:T(8,128)} %get-tuple-element.51, f32[1024]{0:T(1024)S(1)} %add.110, f32[1024,4096]{1,0:T(8,128)} %get-tuple-element.33, f32[1024]{0:T(1024)S(1)} %add.109, f32[1024]{0:T(1024)S(1)} %max.31), kind=kOutput, calls=%fused_computation.44 | convolution fusion | flops 1099956224 | bytes 38023168 | tf_op jit(solution)/shard_map/dot_general | solution.py:82
  262.7 14.0 %fusion.26 = f32[4096,128]{0,1:T(8,128)S(1)} fusion(f32[4096,128]{0,1:T(8,128)S(1)} %copy-done.41, bf16[1024,128]{1,0:T(8,128)(2,1)S(1)} %copy-done.10, f32[1024,4096]{1,0:T(8,128)} %get-tuple-element.55, f32[1024]{0:T(1024)S(1)} %add.105, f32[1024,4096]{1,0:T(8,128)} %get-tuple-element.41, f32[1024]{0:T(1024)S(1)} %copy-done.34, f32[1024]{0:T(1024)S(1)} %copy-done.32), kind=kOutput, calls=%fused_computation.43 | convolution fusion | flops 1099956224 | bytes 38023168 | tf_op jit(solution)/shard_map/dot_general | solution.py:82
  276.7 3.8 pad_maximum_fusion
  280.6 113.3 %reduce-scatter.2.cloned.1.call-done = f32[512,512]{0,1:T(8,128)} async-done(((f32[4096,512]{0,1:T(8,128)}), f32[512,512]{0,1:T(8,128)}) %reduce-scatter.2.cloned.1.call-update) | async-done | bytes 1048592 | tf_op jit(solution)/shard_map/reduce_scatter | solution.py:19
  393.9 1.3 fusion.87
  395.2 0.2 copy.37
  395.4 0.3 copy.43
  395.7 0.2 copy.38
  395.9 0.3 copy.44
  396.2 2.3 broadcast_in_dim.31
  398.5 52.2 %all_to_all.6 = f32[4,1,262144]{2,1,0:T(1,128)} all-to-all(f32[4,1,262144]{2,1,0:T(1,128)S(1)} %broadcast_in_dim.31), channel_id=1, replica_groups=mesh['dp'=8,'tensor'=4,'replica'=4] {'replica'}, dimensions={0} | all-to-all | bytes 8388608 | tf_op jit(solution)/shard_map/all_to_all | solution.py:28
  450.7 9.8 %reduce_sum.169 = f32[262144]{0:T(1024)S(1)} reduce(f32[4,1,262144]{2,1,0:T(1,128)} %all_to_all.6, f32[]{:T(128)} %constant.5.clone.1), dimensions={0,1}, to_apply=%region_25.26 | reduce | flops 786432 | bytes 5242884 | tf_op jit(solution)/shard_map/reduce_sum | solution.py:33
  461.0 3.9 fusion.81
  464.9 0.8 pad_maximum_fusion.2
  465.7 67.6 %all-gather.8.cloned.1.call-done = bf16[4096,512]{1,0:T(8,128)(2,1)} async-done(((bf16[512,512]{1,0:T(8,128)(2,1)}), bf16[4096,512]{1,0:T(8,128)(2,1)}) %all-gather.8.cloned.1.call-update) | async-done | bytes 4194320 | tf_op jit(solution)/shard_map/all_gather | solution.py:50
  533.4 4.5 fusion.85
  (137 shorter events, 1.0 us)
Async XLA Ops:
  7.2 17.0 %copy-start.23 = (bf16[256,256]{1,0:T(8,128)(2,1)S(1)}, bf16[256,256]{1,0:T(8,128)(2,1)}, u32[]{:S(2)}) copy-start(bf16[256,256]{1,0:T(8,128)(2,1)} %param.13) | copy-start | bytes 393220
  7.2 61.4 %all-gather.4.cloned.1.call-start = ((), (), s32[]{:S(2)}) async-start(), calls=%async_computation.2 | async-start | bytes 2359296 | tf_op jit(solution)/shard_map/all_gather | solution.py:147
  9.1 165.5 %all-gather.6.cloned.1.call-start = ((), (), s32[]{:S(2)}) async-start(), calls=%async_computation.3 | async-start | bytes 2359296 | tf_op jit(solution)/shard_map/all_gather | solution.py:148
  10.9 383.0 %reduce-scatter.2.cloned.1.call-start = ((), (), s32[]{:S(2)}) async-start(), calls=%async_computation.4 | async-start | bytes 9437184 | tf_op jit(solution)/shard_map/reduce_scatter | solution.py:19
  14.1 122.9 %copy-start.13 = (bf16[1024,128]{1,0:T(8,128)(2,1)}, bf16[1024,128]{1,0:T(8,128)(2,1)S(1)}, u32[]{:S(2)}) copy-start(bf16[1024,128]{1,0:T(8,128)(2,1)S(1)} %reshape.191) | copy-start | bytes 786436
  14.3 90.1 %copy-start.9 = (bf16[1024,128]{1,0:T(8,128)(2,1)}, bf16[1024,128]{1,0:T(8,128)(2,1)S(1)}, u32[]{:S(2)}) copy-start(bf16[1024,128]{1,0:T(8,128)(2,1)S(1)} %reshape.193) | copy-start | bytes 786436
  14.5 72.7 %copy-start.11 = (bf16[1024,128]{1,0:T(8,128)(2,1)}, bf16[1024,128]{1,0:T(8,128)(2,1)S(1)}, u32[]{:S(2)}) copy-start(bf16[1024,128]{1,0:T(8,128)(2,1)S(1)} %reshape.197) | copy-start | bytes 786436
  14.6 4.8 copy-start.15
  20.7 66.5 %copy-start.2 = (f32[1024,256]{0,1:T(8,128)}, f32[1024,256]{0,1:T(8,128)S(1)}, u32[]{:S(2)}) copy-start(f32[1024,256]{0,1:T(8,128)S(1)} %get-tuple-element.39) | copy-start | bytes 3145732
  21.9 73.4 %copy-start.4 = (f32[1024,256]{0,1:T(8,128)}, f32[1024,256]{0,1:T(8,128)S(1)}, u32[]{:S(2)}) copy-start(f32[1024,256]{0,1:T(8,128)S(1)} %get-tuple-element.35) | copy-start | bytes 3145732
  68.6 18.6 %copy-start = (bf16[4096,256]{1,0:T(8,128)(2,1)S(1)}, bf16[4096,256]{1,0:T(8,128)(2,1)}, u32[]{:S(2)}) copy-start(bf16[4096,256]{1,0:T(8,128)(2,1)} %all-gather.4.cloned.1.call-done) | copy-start | bytes 6291460
  95.5 17.1 %copy-start.6 = (f32[1024,256]{0,1:T(8,128)S(1)}, f32[1024,256]{0,1:T(8,128)}, u32[]{:S(2)}) copy-start(f32[1024,256]{0,1:T(8,128)} %get-tuple-element.43) | copy-start | bytes 3145732
  104.4 17.2 %copy-start.27 = (bf16[1024,128]{1,0:T(8,128)(2,1)S(1)}, bf16[1024,128]{1,0:T(8,128)(2,1)}, u32[]{:S(2)}) copy-start(bf16[1024,128]{1,0:T(8,128)(2,1)} %reshape.198) | copy-start | bytes 786436
  112.5 54.9 %copy-start.31 = (f32[1024]{0:T(1024)}, f32[1024]{0:T(1024)S(1)}, u32[]{:S(2)}) copy-start(f32[1024]{0:T(1024)S(1)} %max.29) | copy-start | bytes 12292
  112.7 18.7 %slice-start = ((s8[16777216]{0:T(1024)(128)(4,1)}), s8[4194304]{0:T(1024)(128)(4,1)S(1)}, s32[]{:S(2)}) async-start(s8[16777216]{0:T(1024)(128)(4,1)} %bitcast.29), calls=%async_computation.6 | async-start | bytes 8388608
  121.6 9.8 %slice-start.1 = ((s8[16777216]{0:T(1024)(128)(4,1)}), s8[4194304]{0:T(1024)(128)(4,1)S(1)}, s32[]{:S(2)}) async-start(s8[16777216]{0:T(1024)(128)(4,1)} %bitcast.29), calls=%async_computation.7 | async-start | bytes 8388608
  121.6 9.8 %slice-start.2 = ((s8[16777216]{0:T(1024)(128)(4,1)}), s8[4194304]{0:T(1024)(128)(4,1)S(1)}, s32[]{:S(2)}) async-start(s8[16777216]{0:T(1024)(128)(4,1)} %bitcast.29), calls=%async_computation.8 | async-start | bytes 8388608
  121.6 10.2 %slice-start.3 = ((s8[16777216]{0:T(1024)(128)(4,1)}), s8[4194304]{0:T(1024)(128)(4,1)S(1)}, s32[]{:S(2)}) async-start(s8[16777216]{0:T(1024)(128)(4,1)} %bitcast.29), calls=%async_computation.9 | async-start | bytes 8388608
  121.6 10.2 %copy-start.24 = (bf16[1024,128]{1,0:T(8,128)(2,1)S(1)}, bf16[1024,128]{1,0:T(8,128)(2,1)}, u32[]{:S(2)}) copy-start(bf16[1024,128]{1,0:T(8,128)(2,1)} %reshape.194) | copy-start | bytes 786436
  131.8 35.6 %copy-start.33 = (f32[1024]{0:T(1024)}, f32[1024]{0:T(1024)S(1)}, u32[]{:S(2)}) copy-start(f32[1024]{0:T(1024)S(1)} %add.104) | copy-start | bytes 12292
  131.8 5.2 copy-start.1
  145.1 24.1 %slice-start.4 = ((s8[16777216]{0:T(1024)(128)(4,1)}), s8[4194304]{0:T(1024)(128)(4,1)S(1)}, s32[]{:S(2)}) async-start(s8[16777216]{0:T(1024)(128)(4,1)} %bitcast.31), calls=%async_computation.10 | async-start | bytes 8388608
  153.9 12.0 %copy-start.8 = (f32[1024,256]{0,1:T(8,128)S(1)}, f32[1024,256]{0,1:T(8,128)}, u32[]{:S(2)}) copy-start(f32[1024,256]{0,1:T(8,128)} %get-tuple-element.47) | copy-start | bytes 3145732
  153.9 12.2 %copy-start.3 = (f32[1024,256]{0,1:T(8,128)S(1)}, f32[1024,256]{0,1:T(8,128)}, u32[]{:S(2)}) copy-start(f32[1024,256]{0,1:T(8,128)} %copy-done.2) | copy-start | bytes 3145732
  153.9 12.2 %copy-start.29 = (bf16[1024,128]{1,0:T(8,128)(2,1)S(1)}, bf16[1024,128]{1,0:T(8,128)(2,1)}, u32[]{:S(2)}) copy-start(bf16[1024,128]{1,0:T(8,128)(2,1)} %reshape.196) | copy-start | bytes 786436
  153.9 12.2 %copy-start.39 = (bf16[256,256]{1,0:T(8,128)(2,1)S(1)}, bf16[256,256]{1,0:T(8,128)(2,1)}, u32[]{:S(2)}) copy-start(bf16[256,256]{1,0:T(8,128)(2,1)} %param.14) | copy-start | bytes 393220
  153.9 12.5 %copy-start.5 = (f32[1024,256]{0,1:T(8,128)S(1)}, f32[1024,256]{0,1:T(8,128)}, u32[]{:S(2)}) copy-start(f32[1024,256]{0,1:T(8,128)} %copy-done.4) | copy-start | bytes 3145732
  154.0 12.5 %copy-start.28 = (bf16[1024,128]{1,0:T(8,128)(2,1)S(1)}, bf16[1024,128]{1,0:T(8,128)(2,1)}, u32[]{:S(2)}) copy-start(bf16[1024,128]{1,0:T(8,128)(2,1)} %reshape.198) | copy-start | bytes 786436
  154.0 13.4 %copy-start.7 = (f32[1024,256]{0,1:T(8,128)S(1)}, f32[1024,256]{0,1:T(8,128)}, u32[]{:S(2)}) copy-start(f32[1024,256]{0,1:T(8,128)} %get-tuple-element.43) | copy-start | bytes 3145732
  154.0 14.3 %copy-start.26 = (bf16[1024,128]{1,0:T(8,128)(2,1)S(1)}, bf16[1024,128]{1,0:T(8,128)(2,1)}, u32[]{:S(2)}) copy-start(bf16[1024,128]{1,0:T(8,128)(2,1)} %reshape.192) | copy-start | bytes 786436
  154.0 15.2 %slice-start.5 = ((s8[16777216]{0:T(1024)(128)(4,1)}), s8[4194304]{0:T(1024)(128)(4,1)S(1)}, s32[]{:S(2)}) async-start(s8[16777216]{0:T(1024)(128)(4,1)} %bitcast.31), calls=%async_computation.11 | async-start | bytes 8388608
  154.0 15.2 %slice-start.6 = ((s8[16777216]{0:T(1024)(128)(4,1)}), s8[4194304]{0:T(1024)(128)(4,1)S(1)}, s32[]{:S(2)}) async-start(s8[16777216]{0:T(1024)(128)(4,1)} %bitcast.31), calls=%async_computation.12 | async-start | bytes 8388608
  154.0 15.2 %slice-start.7 = ((s8[16777216]{0:T(1024)(128)(4,1)}), s8[4194304]{0:T(1024)(128)(4,1)S(1)}, s32[]{:S(2)}) async-start(s8[16777216]{0:T(1024)(128)(4,1)} %bitcast.31), calls=%async_computation.13 | async-start | bytes 8388608
  165.9 3.3 copy-start.42
  169.3 5.3 copy-start.30
  174.6 11.8 %copy-start.16 = (bf16[1024,128]{1,0:T(8,128)(2,1)S(1)}, bf16[1024,128]{1,0:T(8,128)(2,1)}, u32[]{:S(2)}) copy-start(bf16[1024,128]{1,0:T(8,128)(2,1)} %copy-done.15) | copy-start | bytes 786436
  186.4 26.8 %slice-start.8 = ((s8[16777216]{0:T(1024)(128)(4,1)}), s8[4194304]{0:T(1024)(128)(4,1)S(1)}, s32[]{:S(2)}) async-start(s8[16777216]{0:T(1024)(128)(4,1)} %bitcast.33), calls=%async_computation.14 | async-start | bytes 8388608
  186.4 26.8 %slice-start.9 = ((s8[16777216]{0:T(1024)(128)(4,1)}), s8[4194304]{0:T(1024)(128)(4,1)S(1)}, s32[]{:S(2)}) async-start(s8[16777216]{0:T(1024)(128)(4,1)} %bitcast.33), calls=%async_computation.15 | async-start | bytes 8388608
  186.4 26.8 %slice-start.10 = ((s8[16777216]{0:T(1024)(128)(4,1)}), s8[4194304]{0:T(1024)(128)(4,1)S(1)}, s32[]{:S(2)}) async-start(s8[16777216]{0:T(1024)(128)(4,1)} %bitcast.33), calls=%async_computation.16 | async-start | bytes 8388608
  201.1 12.0 %copy-start.37 = (f32[1024]{0:T(1024)S(1)}, f32[1024]{0:T(1024)}, u32[]{:S(2)}) copy-start(f32[1024]{0:T(1024)} %fusion.41) | copy-start | bytes 12292
  201.1 12.1 %slice-start.11 = ((s8[16777216]{0:T(1024)(128)(4,1)}), s8[4194304]{0:T(1024)(128)(4,1)S(1)}, s32[]{:S(2)}) async-start(s8[16777216]{0:T(1024)(128)(4,1)} %bitcast.33), calls=%async_computation.17 | async-start | bytes 8388608
  213.2 9.3 %copy-start.36 = (f32[1024]{0:T(1024)S(1)}, f32[1024]{0:T(1024)}, u32[]{:S(2)}) copy-start(f32[1024]{0:T(1024)} %fusion.38) | copy-start | bytes 12292
  213.2 9.3 %copy-start.14 = (bf16[1024,128]{1,0:T(8,128)(2,1)S(1)}, bf16[1024,128]{1,0:T(8,128)(2,1)}, u32[]{:S(2)}) copy-start(bf16[1024,128]{1,0:T(8,128)(2,1)} %copy-done.13) | copy-start | bytes 786436
  222.5 14.8 %copy-start.25 = (bf16[1024,128]{1,0:T(8,128)(2,1)S(1)}, bf16[1024,128]{1,0:T(8,128)(2,1)}, u32[]{:S(2)}) copy-start(bf16[1024,128]{1,0:T(8,128)(2,1)} %reshape.194) | copy-start | bytes 786436
  222.5 14.7 %copy-start.32 = (f32[1024]{0:T(1024)S(1)}, f32[1024]{0:T(1024)}, u32[]{:S(2)}) copy-start(f32[1024]{0:T(1024)} %copy-done.31) | copy-start | bytes 12292
  222.6 14.7 %copy-start.34 = (f32[1024]{0:T(1024)S(1)}, f32[1024]{0:T(1024)}, u32[]{:S(2)}) copy-start(f32[1024]{0:T(1024)} %copy-done.33) | copy-start | bytes 12292
  222.6 14.7 %copy-start.38 = (bf16[4096,256]{1,0:T(8,128)(2,1)S(1)}, bf16[4096,256]{1,0:T(8,128)(2,1)}, u32[]{:S(2)}) copy-start(bf16[4096,256]{1,0:T(8,128)(2,1)} %all-gather.6.cloned.1.call-done) | copy-start | bytes 6291460
  237.3 11.7 %copy-start.35 = (f32[1024]{0:T(1024)S(1)}, f32[1024]{0:T(1024)}, u32[]{:S(2)}) copy-start(f32[1024]{0:T(1024)} %fusion.39) | copy-start | bytes 12292
  237.3 11.7 %copy-start.12 = (bf16[1024,128]{1,0:T(8,128)(2,1)S(1)}, bf16[1024,128]{1,0:T(8,128)(2,1)}, u32[]{:S(2)}) copy-start(bf16[1024,128]{1,0:T(8,128)(2,1)} %copy-done.11) | copy-start | bytes 786436
  237.3 11.7 %copy-start.40 = (f32[4096,128]{0,1:T(8,128)S(1)}, f32[4096,128]{0,1:T(8,128)}, u32[]{:S(2)}) copy-start(f32[4096,128]{0,1:T(8,128)} %fusion.10) | copy-start | bytes 6291460
  249.0 13.7 %copy-start.10 = (bf16[1024,128]{1,0:T(8,128)(2,1)S(1)}, bf16[1024,128]{1,0:T(8,128)(2,1)}, u32[]{:S(2)}) copy-start(bf16[1024,128]{1,0:T(8,128)(2,1)} %copy-done.9) | copy-start | bytes 786436
  249.0 13.7 %copy-start.41 = (f32[4096,128]{0,1:T(8,128)S(1)}, f32[4096,128]{0,1:T(8,128)}, u32[]{:S(2)}) copy-start(f32[4096,128]{0,1:T(8,128)} %fusion.8) | copy-start | bytes 6291460
  262.7 14.0 %copy-start.17 = (f32[4096,128]{0,1:T(8,128)S(1)}, f32[4096,128]{0,1:T(8,128)}, u32[]{:S(2)}) copy-start(f32[4096,128]{0,1:T(8,128)} %fusion.31) | copy-start | bytes 6291460
  262.7 14.0 %copy-start.18 = (f32[4096,128]{0,1:T(8,128)S(1)}, f32[4096,128]{0,1:T(8,128)}, u32[]{:S(2)}) copy-start(f32[4096,128]{0,1:T(8,128)} %fusion.28) | copy-start | bytes 6291460
  280.5 180.4 %copy-start.19 = (f32[512,256]{1,0:T(8,128)S(1)}, f32[512,256]{1,0:T(8,128)}, u32[]{:S(2)}) copy-start(f32[512,256]{1,0:T(8,128)} %param.16) | copy-start | bytes 1572868
  280.5 180.4 %copy-start.20 = (f32[512,256]{1,0:T(8,128)S(1)}, f32[512,256]{1,0:T(8,128)}, u32[]{:S(2)}) copy-start(f32[512,256]{1,0:T(8,128)} %param.17) | copy-start | bytes 1572868
  280.5 252.8 %all-gather.8.cloned.1.call-start = ((), (), s32[]{:S(2)}) async-start(), calls=%async_computation.5 | async-start | bytes 4718592 | tf_op jit(solution)/shard_map/all_gather | solution.py:50
  460.8 77.1 %copy-start.21 = (f32[512,256]{1,0:T(8,128)}, f32[512,256]{1,0:T(8,128)S(1)}, u32[]{:S(2)}) copy-start(f32[512,256]{1,0:T(8,128)S(1)} %slice.109) | copy-start | bytes 1572868
  461.0 76.9 %copy-start.22 = (f32[512,256]{1,0:T(8,128)}, f32[512,256]{1,0:T(8,128)S(1)}, u32[]{:S(2)}) copy-start(f32[512,256]{1,0:T(8,128)S(1)} %slice.107) | copy-start | bytes 1572868
Sparse Core Ops, SparseCore 0:
  10.9 57.6 all-gather.3
  71.5 53.7 all-gather.5
  280.6 113.2 reduce-scatter.1
  465.8 67.4 all-gather.7
where the time goes:
time: 554 us; the launch traced here: 545 us
  waiting for transfers between devices  224 us (40%)
  matrix products  177 us (32%)
  other arithmetic  59 us (11%)
  blocking collectives  52.2 us (9%)
  local copies, waits for them, and re-layouts  17.6 us (3%)
  between operations  15 us (3%)
    reduce_scatter x1, waiting for transfers between devices, sent_together(): lax.psum_scatter(both, axis, scatter_dimension=dim, tiled=True)  113 us
    all_gather x1, waiting for transfers between devices, side_by_side(): lax.all_gather(both, axis, axis=dim, tiled=True)  67.6 us
    dot_general x4, matrix products, attend_block(): lax.dot_general(cart_dscore, flat_query, contract, preferred_element_type...  57.1 us
    all_to_all x1, blocking collectives, from_everyone(): return lax.all_to_all(copies, axis, split_axis=0, concat_axis=0, tiled=True)  52.2 us
    dot_general x4, matrix products, attend_block(): jnp.dot(flat_grad, cart_values.T, preferred_element_type=jnp.float32)  44.7 us
    all_gather x1, waiting for transfers between devices, per_device(): lax.all_gather(master_keys.astype(jnp.bfloat16), 'dp', axis=0, tiled=True)  43.1 us
    reduce_sum x4, other arithmetic, attend_block(): jnp.sum(cart_exp, axis=1, keepdims=True)  35.5 us
    dot_general x4, matrix products, attend_block(): jnp.dot(flat_query, cart_keys.T, preferred_element_type=jnp.float32)  33.8 us
  transfers between devices with their start and end apart: 4, of which 3 were waited for; matrix products, arithmetic and copies ran while one was open for 22% of the time, Pallas kernels for 0%

commit v1 on v0

--- a/solution.py
+++ b/solution.py
@@ -12,6 +12,12 @@
 LEARN_RATE = 0.05
 WEIGHT_DECAY = 0.1
 EPSILON = 1e-08
+find_zones = lambda field: jnp.concatenate(
+    lax.all_to_all(
+        jnp.stack(lax.axis_size("dp") * [field]), axis_name="dp", split_axis=0, concat_axis=0
+    ),
+    axis=0,
+)
 
 
 def sent_together(arrays, axis, dim, along):
@@ -144,7 +150,7 @@
     second_values,
 ):
     cart_keys, cart_values = (
-        lax.all_gather(master_keys.astype(jnp.bfloat16), "dp", axis=0, tiled=True),
+        find_zones(master_keys.astype(jnp.bfloat16)),
         lax.all_gather(master_values.astype(jnp.bfloat16), "dp", axis=0, tiled=True),
     )
     grad_keys, grad_values = device_grads(

time: 554 us -> 537 us (0.969)
  waiting for transfers between devices: 224 us -> 188 us
  local copies, waits for them, and re-layouts: 17.6 us -> 26.5 us
  starting transfers between devices: 0.16 us -> 8.02 us
    all_gather x1 -> x0, waiting for transfers between devices: 43.1 us -> none  [per_device(): lax.all_gather(master_keys.astype(jnp.bfloat16), 'dp', axis=0, tiled=True)]
    all_to_all x0 -> x1, starting transfers between devices: none -> 7.89 us  [lax.all_to_all(jnp.stack(lax.axis_size('dp') * [field]), axis_name='dp',...]
  transfers between devices with their start and end apart: 4 -> 4, of which waited for: 3 -> 3; matrix products, arithmetic and copies ran while one was open for 22% -> 25% of each run, Pallas kernels for 0% -> 0%
where the time goes in v1:
time: 537 us; the launch traced here: 527 us
  waiting for transfers between devices  188 us (35%)
  matrix products  179 us (33%)
  other arithmetic  58.9 us (11%)
  blocking collectives  52.2 us (10%)
  local copies, waits for them, and re-layouts  26.5 us (5%)
  between operations  14.7 us (3%)
  starting transfers between devices  8.02 us (1%)
    reduce_scatter x1, waiting for transfers between devices, sent_together(): lax.psum_scatter(both, axis, scatter_dimension=dim, tiled=True)  116 us
    all_gather x1, waiting for transfers between devices, side_by_side(): lax.all_gather(both, axis, axis=dim, tiled=True)  67.6 us
    dot_general x4, matrix products, attend_block(): lax.dot_general(cart_dscore, flat_query, contract, preferred_element_type...  57.3 us
    all_to_all x1, blocking collectives, from_everyone(): return lax.all_to_all(copies, axis, split_axis=0, concat_axis=0, tiled=True)  52.2 us
    dot_general x4, matrix products, attend_block(): jnp.dot(flat_grad, cart_values.T, preferred_element_type=jnp.float32)  44.5 us
    reduce_sum x4, other arithmetic, attend_block(): jnp.sum(cart_exp, axis=1, keepdims=True)  34.9 us
    dot_general x4, matrix products, attend_block(): jnp.dot(flat_query, cart_keys.T, preferred_element_type=jnp.float32)  33.9 us
    dot_general x4, matrix products, attend_block(): lax.dot_general(cart_probs.astype(jnp.bfloat16), flat_grad, contract, pre...  31.9 us
  transfers between devices with their start and end apart: 4, of which 3 were waited for; matrix products, arithmetic and copies ran while one was open for 25% of the time, Pallas kernels for 0%

profile of v1, /device:TPU:0, one launch (start us, length us, event | category | flops | bytes accessed | tf_op | source)
XLA Modules:
  0.0 527.1 jit_solution(4726103808294323209)
XLA Ops:
  7.2 1.1 convert_element_type.36
  8.3 1.5 stack.2
  9.8 7.9 %all-to-all-start = ((bf16[8,512,256]{2,1,0:T(8,128)(2,1)}), bf16[8,512,256]{2,1,0:T(8,128)(2,1)S(1)}, u32[]{:S(2)}, u32[]{:S(2)}) async-start(bf16[8,512,256]{2,1,0:T(8,128)(2,1)} %stack.2), calls=%async_computation | async-start | bytes 4194304 | tf_op jit(solution)/shard_map/all_to_all | solution.py:16
  17.7 1.8 convert_element_type.37
  19.5 2.0 fusion.89
  21.5 0.9 reshape.204
  22.4 2.1 fusion.88
  24.4 0.9 reshape.203
  25.3 0.9 fusion.64
  26.2 0.2 broadcast_in_dim.28
  26.4 0.2 broadcast_in_dim.29
  26.6 0.3 copy.33
  27.0 1.8 reshape.202
  28.8 1.8 reshape.201
  30.6 0.9 reshape.200
  31.5 1.8 reshape.199
  33.3 0.9 reshape.198
  34.2 0.9 reshape.196
  35.1 1.3 fusion.90
  36.4 2.5 fusion.91
  38.8 2.3 fusion.92
  41.1 2.3 fusion.93
  43.4 4.5 all-to-all-done
  47.8 9.1 %multiply_reduce_fusion.4 = (f32[1024]{0:T(1024)S(1)}, f32[1024,4096]{1,0:T(8,128)}) fusion(bf16[1024,128]{1,0:T(8,128)(2,1)} %reshape.203, bf16[4096,256]{1,0:T(8,128)(2,1)S(1)} %bitcast.36), kind=kOutput, calls=%fused_computation.12 | convolution fusion | flops 1082129408 | bytes 18092032 | tf_op jit(solution)/shard_map/dot_general | solution.py:65
  56.9 8.2 %multiply_reduce_fusion.5 = (f32[1024]{0:T(1024)S(1)}, f32[1024,4096]{1,0:T(8,128)}) fusion(bf16[1024,128]{1,0:T(8,128)(2,1)S(1)} %copy-done.11, bf16[4096,256]{1,0:T(8,128)(2,1)S(1)} %bitcast.37), kind=kOutput, calls=%fused_computation.13 | convolution fusion | flops 1082129408 | bytes 18092032 | tf_op jit(solution)/shard_map/dot_general | solution.py:65
  65.1 8.1 %multiply_reduce_fusion.6 = (f32[1024]{0:T(1024)S(1)}, f32[1024,4096]{1,0:T(8,128)}) fusion(bf16[1024,128]{1,0:T(8,128)(2,1)S(1)} %copy-done.7, bf16[4096,256]{1,0:T(8,128)(2,1)S(1)} %bitcast.38), kind=kOutput, calls=%fused_computation.14 | convolution fusion | flops 1082129408 | bytes 18092032 | tf_op jit(solution)/shard_map/dot_general | solution.py:65
  73.2 8.6 %multiply_reduce_fusion.7 = (f32[1024]{0:T(1024)S(1)}, f32[1024,4096]{1,0:T(8,128)}) fusion(bf16[1024,128]{1,0:T(8,128)(2,1)S(1)} %copy-done.9, bf16[4096,256]{1,0:T(8,128)(2,1)S(1)} %bitcast.39), kind=kOutput, calls=%fused_computation.15 | convolution fusion | flops 1082129408 | bytes 18092032 | tf_op jit(solution)/shard_map/dot_general | solution.py:65
  81.7 8.7 %fusion.7 = f32[1024]{0:T(1024)S(1)} fusion(f32[1024,4096]{1,0:T(8,128)} %get-tuple-element.33, f32[1024]{0:T(1024)S(1)} %max.31), kind=kLoop, calls=%fused_computation.23 | loop fusion | flops 12581888 | bytes 16785408 | tf_op jit(solution)/shard_map/reduce_sum | solution.py:74
  90.7 8.7 %fusion.5 = f32[1024]{0:T(1024)S(1)} fusion(f32[1024,4096]{1,0:T(8,128)} %get-tuple-element.37, f32[1024]{0:T(1024)S(1)} %max.30), kind=kLoop, calls=%fused_computation.21 | loop fusion | flops 12581888 | bytes 16785408 | tf_op jit(solution)/shard_map/reduce_sum | solution.py:74
  99.3 0.2 fusion.44
  99.5 8.8 %fusion.3 = f32[1024]{0:T(1024)S(1)} fusion(f32[1024,4096]{1,0:T(8,128)} %get-tuple-element.41, f32[1024]{0:T(1024)S(1)} %max.29), kind=kLoop, calls=%fused_computation.19 | loop fusion | flops 12581888 | bytes 16785408 | tf_op jit(solution)/shard_map/reduce_sum | solution.py:74
  108.3 1.4 fusion.43
  109.8 9.5 %fusion.12 = f32[4096,128]{0,1:T(8,128)} fusion(bf16[1024,128]{1,0:T(8,128)(2,1)S(1)} %copy-done.22, f32[1024,4096]{1,0:T(8,128)} %get-tuple-element.33, f32[1024]{0:T(1024)S(1)} %add.109, f32[1024]{0:T(1024)S(1)} %max.31), kind=kOutput, calls=%fused_computation.29 | convolution fusion | flops 1090519040 | bytes 19144704 | tf_op jit(solution)/shard_map/dot_general | solution.py:84
  119.3 0.6 slice-done.3
  119.9 5.2 fusion.16
  125.1 8.8 %fusion.1 = f32[1024]{0:T(1024)S(1)} fusion(f32[1024,4096]{1,0:T(8,128)} %get-tuple-element.45, f32[1024]{0:T(1024)S(1)} %max.28), kind=kLoop, calls=%fused_computation.17 | loop fusion | flops 12581888 | bytes 16785408 | tf_op jit(solution)/shard_map/reduce_sum | solution.py:74
  134.0 11.7 %fusion.31 = f32[4096,128]{0,1:T(8,128)} fusion(f32[4096,128]{0,1:T(8,128)} %fusion.12, bf16[1024,128]{1,0:T(8,128)(2,1)} %reshape.202, f32[1024,4096]{1,0:T(8,128)} %get-tuple-element.37, f32[1024]{0:T(1024)S(1)} %add.107, f32[1024]{0:T(1024)S(1)} %max.30), kind=kOutput, calls=%fused_computation.46 | convolution fusion | flops 1091043328 | bytes 21241856 | tf_op jit(solution)/shard_map/dot_general | solution.py:84
  146.0 0.3 fusion.40
  146.3 0.9 fusion.41
  147.2 0.9 fusion.39
  148.1 0.9 fusion.38
  149.1 5.5 %fusion.28 = f32[4096,128]{0,1:T(8,128)} fusion(f32[4096,128]{0,1:T(8,128)S(1)} %copy-done.37, bf16[1024,128]{1,0:T(8,128)(2,1)S(1)} %copy-done.23, f32[1024,4096]{1,0:T(8,128)S(1)} %bitcast.33, f32[1024]{0:T(1024)S(1)} %add.102, f32[1024]{0:T(1024)S(1)} %max.28), kind=kOutput, calls=%fused_computation.45 | convolution fusion | flops 1091043328 | bytes 21241856 | tf_op jit(solution)/shard_map/dot_general | solution.py:84
  154.6 11.8 %multiply_reduce_fusion.1 = (f32[1024]{0:T(1024)S(1)}, f32[1024,4096]{1,0:T(8,128)}) fusion(f32[1024]{0:T(1024)S(1)} %add.107, f32[1024]{0:T(1024)S(1)} %max.30, f32[1024,4096]{1,0:T(8,128)} %get-tuple-element.37, bf16[1024,128]{1,0:T(8,128)(2,1)S(1)} %copy-done.25, bf16[4096,256]{1,0:T(8,128)(2,1)} %all-gather.3.cloned.1.call-done), kind=kOutput, calls=%fused_computation.4 | convolution fusion | flops 1094712320 | bytes 34877440 | tf_op jit(solution)/shard_map/dot_general | solution.py:77
  166.4 14.7 %fusion.10 = f32[4096,128]{0,1:T(8,128)} fusion(bf16[1024,128]{1,0:T(8,128)(2,1)S(1)} %copy-done.12, f32[1024,4096]{1,0:T(8,128)} %get-tuple-element.49, f32[1024]{0:T(1024)S(1)} %add.108, f32[1024,4096]{1,0:T(8,128)} %get-tuple-element.37, f32[1024]{0:T(1024)S(1)} %add.107, f32[1024]{0:T(1024)S(1)} %max.30), kind=kOutput, calls=%fused_computation.26 | convolution fusion | flops 1098907648 | bytes 35926016 | tf_op jit(solution)/shard_map/dot_general | solution.py:88
  181.1 11.8 %multiply_reduce_fusion = (f32[1024]{0:T(1024)S(1)}, f32[1024,4096]{1,0:T(8,128)}) fusion(f32[1024]{0:T(1024)S(1)} %add.109, f32[1024]{0:T(1024)S(1)} %max.31, f32[1024,4096]{1,0:T(8,128)} %get-tuple-element.33, bf16[1024,128]{1,0:T(8,128)(2,1)S(1)} %copy-done.22, bf16[4096,256]{1,0:T(8,128)(2,1)} %all-gather.3.cloned.1.call-done), kind=kOutput, calls=%fused_computation.1 | convolution fusion | flops 1094712320 | bytes 34877440 | tf_op jit(solution)/shard_map/dot_general | solution.py:77
  193.0 9.3 %multiply_reduce_fusion.3 = (f32[1024]{0:T(1024)S(1)}, f32[1024,4096]{1,0:T(8,128)}) fusion(f32[1024]{0:T(1024)S(1)} %add.102, f32[1024]{0:T(1024)S(1)} %max.28, f32[1024,4096]{1,0:T(8,128)S(1)} %bitcast.35, bf16[1024,128]{1,0:T(8,128)(2,1)S(1)} %copy-done.23, bf16[4096,256]{1,0:T(8,128)(2,1)} %all-gather.3.cloned.1.call-done), kind=kOutput, calls=%fused_computation.10 | convolution fusion | flops 1094712320 | bytes 34877440 | tf_op jit(solution)/shard_map/dot_general | solution.py:77
  202.3 15.2 %fusion.8 = f32[4096,128]{0,1:T(8,128)} fusion(bf16[1024,128]{1,0:T(8,128)(2,1)S(1)} %copy-done.10, f32[1024,4096]{1,0:T(8,128)} %get-tuple-element.53, f32[1024]{0:T(1024)S(1)} %add.103, f32[1024,4096]{1,0:T(8,128)} %get-tuple-element.45, f32[1024]{0:T(1024)S(1)} %add.102, f32[1024]{0:T(1024)S(1)} %max.28), kind=kOutput, calls=%fused_computation.24 | convolution fusion | flops 1098907648 | bytes 35926016 | tf_op jit(solution)/shard_map/dot_general | solution.py:88
  217.6 11.6 %multiply_reduce_fusion.2 = (f32[1024]{0:T(1024)S(1)}, f32[1024,4096]{1,0:T(8,128)}) fusion(f32[1024]{0:T(1024)S(1)} %copy-done.29, f32[1024]{0:T(1024)S(1)} %copy-done.27, f32[1024,4096]{1,0:T(8,128)} %get-tuple-element.41, bf16[1024,128]{1,0:T(8,128)(2,1)S(1)} %copy-done.21, bf16[4096,256]{1,0:T(8,128)(2,1)S(1)} %copy-done.33), kind=kOutput, calls=%fused_computation.7 | convolution fusion | flops 1094712320 | bytes 34877440 | tf_op jit(solution)/shard_map/dot_general | solution.py:77
  229.3 13.7 %fusion.27 = f32[4096,128]{0,1:T(8,128)S(1)} fusion(f32[4096,128]{0,1:T(8,128)S(1)} %copy-done.35, bf16[1024,128]{1,0:T(8,128)(2,1)S(1)} %copy-done.6, f32[1024,4096]{1,0:T(8,128)} %get-tuple-element.51, f32[1024]{0:T(1024)S(1)} %add.110, f32[1024,4096]{1,0:T(8,128)} %get-tuple-element.33, f32[1024]{0:T(1024)S(1)} %add.109, f32[1024]{0:T(1024)S(1)} %max.31), kind=kOutput, calls=%fused_computation.44 | convolution fusion | flops 1099956224 | bytes 38023168 | tf_op jit(solution)/shard_map/dot_general | solution.py:88
  243.0 13.7 %fusion.26 = f32[4096,128]{0,1:T(8,128)S(1)} fusion(f32[4096,128]{0,1:T(8,128)S(1)} %copy-done.36, bf16[1024,128]{1,0:T(8,128)(2,1)S(1)} %copy-done.8, f32[1024,4096]{1,0:T(8,128)} %get-tuple-element.55, f32[1024]{0:T(1024)S(1)} %add.105, f32[1024,4096]{1,0:T(8,128)} %get-tuple-element.41, f32[1024]{0:T(1024)S(1)} %copy-done.29, f32[1024]{0:T(1024)S(1)} %copy-done.27), kind=kOutput, calls=%fused_computation.43 | convolution fusion | flops 1099956224 | bytes 38023168 | tf_op jit(solution)/shard_map/dot_general | solution.py:88
  256.7 3.7 pad_maximum_fusion
  260.5 115.7 %reduce-scatter.2.cloned.1.call-done = f32[512,512]{0,1:T(8,128)} async-done(((f32[4096,512]{0,1:T(8,128)}), f32[512,512]{0,1:T(8,128)}) %reduce-scatter.2.cloned.1.call-update) | async-done | bytes 1048592 | tf_op jit(solution)/shard_map/reduce_scatter | solution.py:25
  376.2 1.3 fusion.87
  377.5 0.2 copy.38
  377.7 0.3 copy.44
  378.0 0.2 copy.37
  378.2 0.3 copy.43
  378.6 2.5 broadcast_in_dim.31
  381.0 52.2 %all_to_all.11 = f32[4,1,262144]{2,1,0:T(1,128)} all-to-all(f32[4,1,262144]{2,1,0:T(1,128)S(1)} %broadcast_in_dim.31), channel_id=1, replica_groups=mesh['dp'=8,'tensor'=4,'replica'=4] {'replica'}, dimensions={0} | all-to-all | bytes 8388608 | tf_op jit(solution)/shard_map/all_to_all | solution.py:34
  433.3 9.8 %reduce_sum.169 = f32[262144]{0:T(1024)S(1)} reduce(f32[4,1,262144]{2,1,0:T(1,128)} %all_to_all.11, f32[]{:T(128)} %constant.5.clone.1), dimensions={0,1}, to_apply=%region_25.26 | reduce | flops 786432 | bytes 5242884 | tf_op jit(solution)/shard_map/reduce_sum | solution.py:39
  443.5 3.9 fusion.81
  447.4 0.8 pad_maximum_fusion.2
  448.2 67.6 %all-gather.5.cloned.1.call-done = bf16[4096,512]{1,0:T(8,128)(2,1)} async-done(((bf16[512,512]{1,0:T(8,128)(2,1)}), bf16[4096,512]{1,0:T(8,128)(2,1)}) %all-gather.5.cloned.1.call-update) | async-done | bytes 4194320 | tf_op jit(solution)/shard_map/all_gather | solution.py:56
  515.9 4.5 fusion.85
  (127 shorter events, 1.2 us)
Async XLA Ops:
  7.2 27.9 %copy-start.19 = (bf16[256,256]{1,0:T(8,128)(2,1)S(1)}, bf16[256,256]{1,0:T(8,128)(2,1)}, u32[]{:S(2)}) copy-start(bf16[256,256]{1,0:T(8,128)(2,1)} %param.13) | copy-start | bytes 393220
  9.8 38.1 %all-to-all-start = ((bf16[8,512,256]{2,1,0:T(8,128)(2,1)}), bf16[8,512,256]{2,1,0:T(8,128)(2,1)S(1)}, u32[]{:S(2)}, u32[]{:S(2)}) async-start(bf16[8,512,256]{2,1,0:T(8,128)(2,1)} %stack.2), calls=%async_computation | async-start | bytes 4194304 | tf_op jit(solution)/shard_map/all_to_all | solution.py:16
  17.6 136.9 %all-gather.3.cloned.1.call-start = ((), (), s32[]{:S(2)}) async-start(), calls=%async_computation.3 | async-start | bytes 2359296 | tf_op jit(solution)/shard_map/all_gather | solution.py:154
  19.5 356.8 %reduce-scatter.2.cloned.1.call-start = ((), (), s32[]{:S(2)}) async-start(), calls=%async_computation.4 | async-start | bytes 9437184 | tf_op jit(solution)/shard_map/reduce_scatter | solution.py:25
  36.3 54.1 %copy-start = (f32[1024,256]{0,1:T(8,128)}, f32[1024,256]{0,1:T(8,128)S(1)}, u32[]{:S(2)}) copy-start(f32[1024,256]{0,1:T(8,128)S(1)} %get-tuple-element.35) | copy-start | bytes 3145732
  47.8 9.1 %copy-start.11 = (bf16[1024,128]{1,0:T(8,128)(2,1)S(1)}, bf16[1024,128]{1,0:T(8,128)(2,1)}, u32[]{:S(2)}) copy-start(bf16[1024,128]{1,0:T(8,128)(2,1)} %reshape.201) | copy-start | bytes 786436
  47.8 17.3 %copy-start.7 = (bf16[1024,128]{1,0:T(8,128)(2,1)S(1)}, bf16[1024,128]{1,0:T(8,128)(2,1)}, u32[]{:S(2)}) copy-start(bf16[1024,128]{1,0:T(8,128)(2,1)} %reshape.199) | copy-start | bytes 786436
  56.9 16.2 %copy-start.9 = (bf16[1024,128]{1,0:T(8,128)(2,1)S(1)}, bf16[1024,128]{1,0:T(8,128)(2,1)}, u32[]{:S(2)}) copy-start(bf16[1024,128]{1,0:T(8,128)(2,1)} %reshape.196) | copy-start | bytes 786436
  81.7 17.6 %copy-start.3 = (f32[1024,256]{0,1:T(8,128)S(1)}, f32[1024,256]{0,1:T(8,128)}, u32[]{:S(2)}) copy-start(f32[1024,256]{0,1:T(8,128)} %get-tuple-element.39) | copy-start | bytes 3145732
  90.6 19.1 %copy-start.22 = (bf16[1024,128]{1,0:T(8,128)(2,1)S(1)}, bf16[1024,128]{1,0:T(8,128)(2,1)}, u32[]{:S(2)}) copy-start(bf16[1024,128]{1,0:T(8,128)(2,1)} %reshape.204) | copy-start | bytes 786436
  99.5 47.7 %copy-start.26 = (f32[1024]{0:T(1024)}, f32[1024]{0:T(1024)S(1)}, u32[]{:S(2)}) copy-start(f32[1024]{0:T(1024)S(1)} %max.29) | copy-start | bytes 12292
  99.5 19.7 %slice-start = ((s8[16777216]{0:T(1024)(128)(4,1)}), s8[4194304]{0:T(1024)(128)(4,1)S(1)}, s32[]{:S(2)}) async-start(s8[16777216]{0:T(1024)(128)(4,1)} %bitcast.30), calls=%async_computation.6 | async-start | bytes 8388608
  109.7 9.5 %slice-start.1 = ((s8[16777216]{0:T(1024)(128)(4,1)}), s8[4194304]{0:T(1024)(128)(4,1)S(1)}, s32[]{:S(2)}) async-start(s8[16777216]{0:T(1024)(128)(4,1)} %bitcast.30), calls=%async_computation.7 | async-start | bytes 8388608
  109.7 9.5 %slice-start.2 = ((s8[16777216]{0:T(1024)(128)(4,1)}), s8[4194304]{0:T(1024)(128)(4,1)S(1)}, s32[]{:S(2)}) async-start(s8[16777216]{0:T(1024)(128)(4,1)} %bitcast.30), calls=%async_computation.8 | async-start | bytes 8388608
  109.8 10.2 %slice-start.3 = ((s8[16777216]{0:T(1024)(128)(4,1)}), s8[4194304]{0:T(1024)(128)(4,1)S(1)}, s32[]{:S(2)}) async-start(s8[16777216]{0:T(1024)(128)(4,1)} %bitcast.30), calls=%async_computation.9 | async-start | bytes 8388608
  109.8 10.2 %copy-start.20 = (bf16[1024,128]{1,0:T(8,128)(2,1)S(1)}, bf16[1024,128]{1,0:T(8,128)(2,1)}, u32[]{:S(2)}) copy-start(bf16[1024,128]{1,0:T(8,128)(2,1)} %reshape.200) | copy-start | bytes 786436
  119.9 27.3 %copy-start.28 = (f32[1024]{0:T(1024)}, f32[1024]{0:T(1024)S(1)}, u32[]{:S(2)}) copy-start(f32[1024]{0:T(1024)S(1)} %add.104) | copy-start | bytes 12292
  125.1 23.9 %slice-start.4 = ((s8[16777216]{0:T(1024)(128)(4,1)}), s8[4194304]{0:T(1024)(128)(4,1)S(1)}, s32[]{:S(2)}) async-start(s8[16777216]{0:T(1024)(128)(4,1)} %bitcast.32), calls=%async_computation.10 | async-start | bytes 8388608
  133.9 11.9 %copy-start.5 = (f32[1024,256]{0,1:T(8,128)S(1)}, f32[1024,256]{0,1:T(8,128)}, u32[]{:S(2)}) copy-start(f32[1024,256]{0,1:T(8,128)} %get-tuple-element.47) | copy-start | bytes 3145732
  133.9 12.0 %copy-start.4 = (f32[1024,256]{0,1:T(8,128)S(1)}, f32[1024,256]{0,1:T(8,128)}, u32[]{:S(2)}) copy-start(f32[1024,256]{0,1:T(8,128)} %get-tuple-element.39) | copy-start | bytes 3145732
  133.9 12.0 %copy-start.24 = (bf16[1024,128]{1,0:T(8,128)(2,1)S(1)}, bf16[1024,128]{1,0:T(8,128)(2,1)}, u32[]{:S(2)}) copy-start(bf16[1024,128]{1,0:T(8,128)(2,1)} %reshape.202) | copy-start | bytes 786436
  133.9 12.0 %copy-start.34 = (bf16[256,256]{1,0:T(8,128)(2,1)S(1)}, bf16[256,256]{1,0:T(8,128)(2,1)}, u32[]{:S(2)}) copy-start(bf16[256,256]{1,0:T(8,128)(2,1)} %param.14) | copy-start | bytes 393220
  133.9 12.3 %copy-start.1 = (f32[1024,256]{0,1:T(8,128)S(1)}, f32[1024,256]{0,1:T(8,128)}, u32[]{:S(2)}) copy-start(f32[1024,256]{0,1:T(8,128)} %copy-done) | copy-start | bytes 3145732
  133.9 13.3 %copy-start.2 = (f32[1024,256]{0,1:T(8,128)S(1)}, f32[1024,256]{0,1:T(8,128)}, u32[]{:S(2)}) copy-start(f32[1024,256]{0,1:T(8,128)} %get-tuple-element.43) | copy-start | bytes 3145732
  134.0 14.2 %copy-start.23 = (bf16[1024,128]{1,0:T(8,128)(2,1)S(1)}, bf16[1024,128]{1,0:T(8,128)(2,1)}, u32[]{:S(2)}) copy-start(bf16[1024,128]{1,0:T(8,128)(2,1)} %reshape.198) | copy-start | bytes 786436
  134.0 15.1 %slice-start.5 = ((s8[16777216]{0:T(1024)(128)(4,1)}), s8[4194304]{0:T(1024)(128)(4,1)S(1)}, s32[]{:S(2)}) async-start(s8[16777216]{0:T(1024)(128)(4,1)} %bitcast.32), calls=%async_computation.11 | async-start | bytes 8388608
  134.0 15.1 %slice-start.6 = ((s8[16777216]{0:T(1024)(128)(4,1)}), s8[4194304]{0:T(1024)(128)(4,1)S(1)}, s32[]{:S(2)}) async-start(s8[16777216]{0:T(1024)(128)(4,1)} %bitcast.32), calls=%async_computation.12 | async-start | bytes 8388608
  134.0 15.1 %slice-start.7 = ((s8[16777216]{0:T(1024)(128)(4,1)}), s8[4194304]{0:T(1024)(128)(4,1)S(1)}, s32[]{:S(2)}) async-start(s8[16777216]{0:T(1024)(128)(4,1)} %bitcast.32), calls=%async_computation.13 | async-start | bytes 8388608
  145.7 3.3 copy-start.37
  149.1 5.5 %copy-start.25 = (bf16[1024,128]{1,0:T(8,128)(2,1)S(1)}, bf16[1024,128]{1,0:T(8,128)(2,1)}, u32[]{:S(2)}) copy-start(bf16[1024,128]{1,0:T(8,128)(2,1)} %reshape.202) | copy-start | bytes 786436
  154.6 11.8 %copy-start.12 = (bf16[1024,128]{1,0:T(8,128)(2,1)S(1)}, bf16[1024,128]{1,0:T(8,128)(2,1)}, u32[]{:S(2)}) copy-start(bf16[1024,128]{1,0:T(8,128)(2,1)} %reshape.201) | copy-start | bytes 786436
  166.4 26.6 %slice-start.8 = ((s8[16777216]{0:T(1024)(128)(4,1)}), s8[4194304]{0:T(1024)(128)(4,1)S(1)}, s32[]{:S(2)}) async-start(s8[16777216]{0:T(1024)(128)(4,1)} %bitcast.34), calls=%async_computation.14 | async-start | bytes 8388608
  166.4 26.6 %slice-start.9 = ((s8[16777216]{0:T(1024)(128)(4,1)}), s8[4194304]{0:T(1024)(128)(4,1)S(1)}, s32[]{:S(2)}) async-start(s8[16777216]{0:T(1024)(128)(4,1)} %bitcast.34), calls=%async_computation.15 | async-start | bytes 8388608
  166.4 26.6 %slice-start.10 = ((s8[16777216]{0:T(1024)(128)(4,1)}), s8[4194304]{0:T(1024)(128)(4,1)S(1)}, s32[]{:S(2)}) async-start(s8[16777216]{0:T(1024)(128)(4,1)} %bitcast.34), calls=%async_computation.16 | async-start | bytes 8388608
  181.1 11.8 %copy-start.32 = (f32[1024]{0:T(1024)S(1)}, f32[1024]{0:T(1024)}, u32[]{:S(2)}) copy-start(f32[1024]{0:T(1024)} %fusion.41) | copy-start | bytes 12292
  181.1 11.8 %slice-start.11 = ((s8[16777216]{0:T(1024)(128)(4,1)}), s8[4194304]{0:T(1024)(128)(4,1)S(1)}, s32[]{:S(2)}) async-start(s8[16777216]{0:T(1024)(128)(4,1)} %bitcast.34), calls=%async_computation.17 | async-start | bytes 8388608
  193.0 9.3 %copy-start.31 = (f32[1024]{0:T(1024)S(1)}, f32[1024]{0:T(1024)}, u32[]{:S(2)}) copy-start(f32[1024]{0:T(1024)} %fusion.38) | copy-start | bytes 12292
  193.0 9.3 %copy-start.10 = (bf16[1024,128]{1,0:T(8,128)(2,1)S(1)}, bf16[1024,128]{1,0:T(8,128)(2,1)}, u32[]{:S(2)}) copy-start(bf16[1024,128]{1,0:T(8,128)(2,1)} %reshape.196) | copy-start | bytes 786436
  202.3 15.2 %copy-start.21 = (bf16[1024,128]{1,0:T(8,128)(2,1)S(1)}, bf16[1024,128]{1,0:T(8,128)(2,1)}, u32[]{:S(2)}) copy-start(bf16[1024,128]{1,0:T(8,128)(2,1)} %reshape.200) | copy-start | bytes 786436
  202.3 15.2 %copy-start.27 = (f32[1024]{0:T(1024)S(1)}, f32[1024]{0:T(1024)}, u32[]{:S(2)}) copy-start(f32[1024]{0:T(1024)} %copy-done.26) | copy-start | bytes 12292
  202.3 15.2 %copy-start.29 = (f32[1024]{0:T(1024)S(1)}, f32[1024]{0:T(1024)}, u32[]{:S(2)}) copy-start(f32[1024]{0:T(1024)} %copy-done.28) | copy-start | bytes 12292
  202.3 15.2 %copy-start.33 = (bf16[4096,256]{1,0:T(8,128)(2,1)S(1)}, bf16[4096,256]{1,0:T(8,128)(2,1)}, u32[]{:S(2)}) copy-start(bf16[4096,256]{1,0:T(8,128)(2,1)} %all-gather.3.cloned.1.call-done) | copy-start | bytes 6291460
  217.5 11.7 %copy-start.30 = (f32[1024]{0:T(1024)S(1)}, f32[1024]{0:T(1024)}, u32[]{:S(2)}) copy-start(f32[1024]{0:T(1024)} %fusion.39) | copy-start | bytes 12292
  217.6 11.7 %copy-start.6 = (bf16[1024,128]{1,0:T(8,128)(2,1)S(1)}, bf16[1024,128]{1,0:T(8,128)(2,1)}, u32[]{:S(2)}) copy-start(bf16[1024,128]{1,0:T(8,128)(2,1)} %reshape.203) | copy-start | bytes 786436
  217.6 11.7 %copy-start.35 = (f32[4096,128]{0,1:T(8,128)S(1)}, f32[4096,128]{0,1:T(8,128)}, u32[]{:S(2)}) copy-start(f32[4096,128]{0,1:T(8,128)} %fusion.10) | copy-start | bytes 6291460
  229.2 13.7 %copy-start.8 = (bf16[1024,128]{1,0:T(8,128)(2,1)S(1)}, bf16[1024,128]{1,0:T(8,128)(2,1)}, u32[]{:S(2)}) copy-start(bf16[1024,128]{1,0:T(8,128)(2,1)} %reshape.199) | copy-start | bytes 786436
  229.3 13.7 %copy-start.36 = (f32[4096,128]{0,1:T(8,128)S(1)}, f32[4096,128]{0,1:T(8,128)}, u32[]{:S(2)}) copy-start(f32[4096,128]{0,1:T(8,128)} %fusion.8) | copy-start | bytes 6291460
  243.0 13.7 %copy-start.13 = (f32[4096,128]{0,1:T(8,128)S(1)}, f32[4096,128]{0,1:T(8,128)}, u32[]{:S(2)}) copy-start(f32[4096,128]{0,1:T(8,128)} %fusion.31) | copy-start | bytes 6291460
  243.0 13.7 %copy-start.14 = (f32[4096,128]{0,1:T(8,128)S(1)}, f32[4096,128]{0,1:T(8,128)}, u32[]{:S(2)}) copy-start(f32[4096,128]{0,1:T(8,128)} %fusion.28) | copy-start | bytes 6291460
  260.5 183.0 %copy-start.15 = (f32[512,256]{1,0:T(8,128)S(1)}, f32[512,256]{1,0:T(8,128)}, u32[]{:S(2)}) copy-start(f32[512,256]{1,0:T(8,128)} %param.16) | copy-start | bytes 1572868
  260.5 183.0 %copy-start.16 = (f32[512,256]{1,0:T(8,128)S(1)}, f32[512,256]{1,0:T(8,128)}, u32[]{:S(2)}) copy-start(f32[512,256]{1,0:T(8,128)} %param.17) | copy-start | bytes 1572868
  260.5 255.4 %all-gather.5.cloned.1.call-start = ((), (), s32[]{:S(2)}) async-start(), calls=%async_computation.5 | async-start | bytes 4718592 | tf_op jit(solution)/shard_map/all_gather | solution.py:56
  443.3 77.1 %copy-start.17 = (f32[512,256]{1,0:T(8,128)}, f32[512,256]{1,0:T(8,128)S(1)}, u32[]{:S(2)}) copy-start(f32[512,256]{1,0:T(8,128)S(1)} %slice.107) | copy-start | bytes 1572868
  443.5 76.9 %copy-start.18 = (f32[512,256]{1,0:T(8,128)}, f32[512,256]{1,0:T(8,128)S(1)}, u32[]{:S(2)}) copy-start(f32[512,256]{1,0:T(8,128)S(1)} %slice.109) | copy-start | bytes 1572868
Sparse Core Ops, SparseCore 0:
  20.8 63.7 all-gather.2
  260.6 115.6 reduce-scatter.1
  448.3 67.4 all-gather.4
